TPU v7x, 128 devices: a whole 4x4x4 slice. The times are simulated.
128 devices in a mesh: gx: 8 (over z, core), gy: 16 (over y, x).
Axes of the slice: x: 4, y: 4, z: 4, core: 2. Of those that a mesh axis runs over, the one named last changes fastest.
Arguments:
- tiles: bfloat16 [24576, 128, 128], P(('gx', 'gy')), may hold values from -6 to 6
- tile_rows: int32 [24576], P(('gx', 'gy')), may hold values from 0 to 63, as said below
- tile_cols: int32 [24576], P(('gx', 'gy')), may hold values from 0 to 255
- tile_counts: int32 [128], P(('gx', 'gy')), may hold values from 48 to 192
- block_order: int32 [256], replicated, may hold values from 0 to 255, each once
- sketch: bfloat16 [32768, 128], replicated, may hold values from -6 to 6
Outputs:
- cell_factor: bfloat16 [1048576, 128], P(('gx', 'gy'))
- gene_factor: float32 [32768, 128], P(('gx', 'gy'))
Inputs may be any that keep to these rules, and one draw needn't show every extreme that they name: On each device the live slots (those below its count) hold distinct coordinate pairs (tile_rows, tile_cols) in increasing lexicographic order; later slots are unused. `block_order`: device d along gx+gy owns the gene blocks in entries d * 2 to (d + 1) * 2 - 1.
All inputs are finite; a program needn't handle non-finite values.
Results may differ from a plain program's by a relative error of at most 0.0019.
Values sent between devices are 32-bit elements; how exact they have to be, the bound alone decides.
A program may use at most 192 MiB of HBM per device.

v0:
```python
import math
import jax
import jax.numpy as jnp
from jax import lax
from jax.sharding import PartitionSpec as P

TILE = 128
SKETCH = 128
GENES = 32768
CB_DEV = 64


def on_device(tiles, tile_rows, tile_cols, tile_counts, block_order, sketch):
    live_count = tile_counts[0]
    blocks_total = GENES // TILE
    sketch_blocks = sketch.reshape(blocks_total, TILE, SKETCH)
    width = 16
    turns = (live_count + width - 1) // width

    def take(start):
        tile_block = lax.dynamic_slice_in_dim(tiles, start, width, 0)
        row_block = lax.dynamic_slice_in_dim(tile_rows, start, width, 0)
        col_block = lax.dynamic_slice_in_dim(tile_cols, start, width, 0)
        alive = start + jnp.arange(width, dtype=jnp.int32) < live_count
        return (tile_block, row_block, col_block, alive)

    def cell_step(turn, total):
        tile_block, row_block, col_block, alive = take(turn * width)
        product = jnp.einsum(
            "tij,tjs->tis", tile_block, sketch_blocks[col_block], preferred_element_type=jnp.float32
        )
        product = jnp.where(alive[:, None, None], product, 0.0)
        return total.at[row_block].add(product)

    cell_sum = lax.fori_loop(0, turns, cell_step, jnp.zeros((CB_DEV, TILE, SKETCH), jnp.float32))
    cell_sum = cell_sum.reshape(CB_DEV * TILE, SKETCH)
    local_gram = jnp.dot(
        cell_sum.T, cell_sum, precision=lax.Precision.HIGHEST, preferred_element_type=jnp.float32
    )
    gram = lax.psum(local_gram, ("gx", "gy"))
    cells_all = CB_DEV * TILE * lax.axis_size("gx") * lax.axis_size("gy")
    lower = jnp.linalg.cholesky(gram)
    cell_factor = (
        math.sqrt(cells_all)
        * lax.linalg.triangular_solve(
            lower, cell_sum, left_side=False, lower=True, transpose_a=True
        )
    ).astype(jnp.bfloat16)
    cell_blocks = cell_factor.reshape(CB_DEV, TILE, SKETCH)

    def gene_step(turn, total):
        tile_block, row_block, col_block, alive = take(turn * width)
        product = jnp.einsum(
            "tji,tjs->tis", tile_block, cell_blocks[row_block], preferred_element_type=jnp.float32
        )
        product = jnp.where(alive[:, None, None], product, 0.0)
        return total.at[col_block].add(product)

    gene_sum = lax.fori_loop(
        0, turns, gene_step, jnp.zeros((blocks_total, TILE, SKETCH), jnp.float32)
    )
    ordered = gene_sum[block_order].reshape(GENES, SKETCH)
    owned = lax.psum_scatter(ordered, ("gx", "gy"), scatter_dimension=0, tiled=True)
    gene_gram = lax.psum(
        jnp.dot(
            owned.T, owned, precision=lax.Precision.HIGHEST, preferred_element_type=jnp.float32
        ),
        ("gx", "gy"),
    )
    lower_genes = jnp.linalg.cholesky(gene_gram)
    gene_factor = math.sqrt(GENES) * lax.linalg.triangular_solve(
        lower_genes, owned, left_side=False, lower=True, transpose_a=True
    )
    return (cell_factor, gene_factor)


def solution(mesh):
    placed = (
        P(("gx", "gy"), None, None),
        P(("gx", "gy")),
        P(("gx", "gy")),
        P(("gx", "gy")),
        P(),
        P(),
    )
    return jax.shard_map(
        on_device,
        mesh=mesh,
        in_specs=placed,
        out_specs=(P(("gx", "gy"), None), P(("gx", "gy"), None)),
        check_vma=False,
    )
```

profile of v0, /device:TPU:1, one launch (start us, length us, event | category | flops | bytes accessed | tf_op | source)
XLA Modules:
  0.0 1278.8 jit_solution(311369099258729333)
XLA Ops:
  7.9 2.4 broadcast_in_dim.44
  10.3 47.0 %while.20 = (s32[]{:T(128)}, f32[64,128,128]{2,1,0:T(8,128)}, s32[]{:T(128)}, s32[192]{0:T(256)S(1)}, s32[]{:T(128)}, /*index=5*/bf16[192,128,128]{2,1,0:T(8,128...) while((s32[]{:T(128)}, f32[64,128,128]{2,1,0:T(8,128)}, ...), condition=%wide.region_2.3_spmd, body=%wide.region_0.2_spmd.sunk | while | flops 67634312 | bytes 6296211 | solution.py:35
  10.4 4.0 gather_fusion
  15.1 1.3 convolution_select_fusion.4
  16.5 3.4 scatter_fusion
  19.9 4.0 gather_fusion
  24.6 1.3 convolution_select_fusion.4
  25.9 3.3 scatter_fusion
  29.3 4.0 gather_fusion
  34.0 1.3 convolution_select_fusion.4
  35.3 3.2 scatter_fusion
  38.6 4.0 gather_fusion
  43.3 1.3 convolution_select_fusion.4
  44.7 3.3 scatter_fusion
  48.0 4.0 gather_fusion
  52.7 1.3 convolution_select_fusion.4
  54.1 3.3 scatter_fusion
  57.4 10.8 convolution_bitcast_fusion
  68.5 208.9 %all-reduce.3.cloned.1.call-done = f32[128,128]{0,1:T(8,128)} async-done(((f32[128,128]{0,1:T(8,128)}), f32[128,128]{0,1:T(8,128)}) %all-reduce.3.cloned.1.call-update) | async-done | bytes 65552 | tf_op jit(solution)/shard_map/psum | solution.py:40
  277.4 0.9 copy.10
  279.2 11.7 cholesky.44
  292.2 9.8 custom-call.8
  302.0 6.2 fusion.4
  308.2 7.8 broadcast_in_dim.45
  316.0 39.0 %while.21 = (s32[]{:T(128)}, f32[256,128,128]{2,1,0:T(8,128)}, s32[]{:T(128)}, s32[192]{0:T(256)S(1)}, s32[]{:T(128)}, /*index=5*/bf16[192,128,128]{2,1,0:T(8,12...) while((s32[]{:T(128)}, f32[256,128,128]{2,1,0:T(8,128)}, ...), condition=%wide.region_8.10_spmd, body=%wide.region_6.9_spmd.sunk | while | flops 67634312 | bytes 6296211 | solution.py:59
  316.1 2.2 gather_fusion.1
  319.0 1.4 convolution_select_fusion.5
  320.4 3.4 scatter_fusion.1
  323.9 2.2 gather_fusion.1
  326.8 1.4 convolution_select_fusion.5
  328.2 3.4 scatter_fusion.1
  331.7 2.2 gather_fusion.1
  334.6 1.4 convolution_select_fusion.5
  336.0 3.4 scatter_fusion.1
  339.5 2.2 gather_fusion.1
  342.4 1.4 convolution_select_fusion.5
  343.8 3.4 scatter_fusion.1
  347.2 2.2 gather_fusion.1
  350.2 1.4 convolution_select_fusion.5
  351.6 3.4 scatter_fusion.1
  355.0 17.7 %gather_fusion.2 = f32[256,128,128]{2,1,0:T(8,128)} fusion(f32[256,128,128]{2,1,0:T(8,128)} %get-tuple-element.90, s32[1024]{0:T(1024)S(1)} %pad_clamp_fusion.2), kind=kCustom, calls=%fused_computation.2 | custom fusion | bytes 33555456 | tf_op jit(solution)/shard_map/gather | solution.py:62
  372.7 702.3 %reduce-scatter.2.cloned.1.call-done = f32[256,128]{1,0:T(8,128)} async-done(((f32[32768,128]{1,0:T(8,128)}), f32[256,128]{1,0:T(8,128)}) %reduce-scatter.2.cloned.1.call-update) | async-done | bytes 131088 | tf_op jit(solution)/shard_map/reduce_scatter | solution.py:63
  1075.0 2.0 fusion.11
  1077.0 168.8 %all-reduce.5.cloned.1.call-done = f32[128,128]{0,1:T(8,128)} async-done(((f32[128,128]{0,1:T(8,128)}), f32[128,128]{0,1:T(8,128)}) %all-reduce.5.cloned.1.call-update) | async-done | bytes 65552 | tf_op jit(solution)/shard_map/psum | solution.py:64
  1245.8 0.9 copy.13
  1247.6 11.7 cholesky.55
  1260.7 9.8 custom-call.9
  1270.5 1.8 convolution_multiply_fusion.1
  (52 shorter events, 12.1 us)
Async XLA Ops:
  7.2 3.2 copy-start
  7.2 3.2 copy-start.1
  7.2 270.2 %all-reduce.3.cloned.1.call-start = ((), (), s32[]{:S(2)}) async-start(), calls=%async_computation.1 | async-start | bytes 131072 | tf_op jit(solution)/shard_map/psum | solution.py:40
  57.4 11.1 copy-start.2
  68.2 1006.8 %reduce-scatter.2.cloned.1.call-start = ((), (), s32[]{:S(2)}) async-start(), calls=%async_computation.2 | async-start | bytes 16908288 | tf_op jit(solution)/shard_map/reduce_scatter | solution.py:63
  372.7 873.2 %all-reduce.5.cloned.1.call-start = ((), (), s32[]{:S(2)}) async-start(), calls=%async_computation.3 | async-start | bytes 131072 | tf_op jit(solution)/shard_map/psum | solution.py:64
Sparse Core Ops, SparseCore 0:
  68.3 208.9 all-reduce.2
  372.8 702.1 reduce-scatter.1
  1080.3 165.4 all-reduce.4
where the time goes:
time: 1280 us
  waiting for transfers between devices  1080 us (84%)
  other arithmetic  88.2 us (7%)
  local copies, waits for them, and re-layouts  61.1 us (5%)
  matrix products  34.5 us (3%)
  between operations  14.5 us (1%)
    reduce_scatter x1, waiting for transfers between devices, on_device(): lax.psum_scatter(ordered, ('gx', 'gy'), scatter_dimension=0, tiled=True)  702 us
    psum x1, waiting for transfers between devices, on_device(): gram = lax.psum(local_gram, ('gx', 'gy'))  209 us
    psum x1, waiting for transfers between devices, on_device(): lax.psum(jnp.dot(owned.T, owned, precision=lax.Precision.HIGHEST, preferr...  169 us
  transfers between devices with their start and end apart: 3, of which 3 were waited for; matrix products, arithmetic and copies ran while one was open for 0% of the time, Pallas kernels for 0%

commit v1 on v0

--- a/solution.py
+++ b/solution.py
@@ -37,7 +37,8 @@
     local_gram = jnp.dot(
         cell_sum.T, cell_sum, precision=lax.Precision.HIGHEST, preferred_element_type=jnp.float32
     )
-    gram = lax.psum(local_gram, ("gx", "gy"))
+    terms = lax.all_gather(local_gram, ("gx", "gy"), axis=0, tiled=False)
+    gram = terms.sum(axis=0)
     cells_all = CB_DEV * TILE * lax.axis_size("gx") * lax.axis_size("gy")
     lower = jnp.linalg.cholesky(gram)
     cell_factor = (

time: 1280 us -> 1220 us (0.953)
  waiting for transfers between devices: 1080 us -> 1010 us
    psum x1 -> x0, waiting for transfers between devices: 209 us -> none  [on_device(): gram = lax.psum(local_gram, ('gx', 'gy'))]
    all_gather x0 -> x1, waiting for transfers between devices: none -> 140 us  [on_device(): terms = lax.all_gather(local_gram, ('gx', 'gy'), axis=0, tiled=False)]
where the time goes in v1:
time: 1220 us; the launch traced here: 1210 us
  waiting for transfers between devices  1010 us (83%)
  other arithmetic  91.1 us (7%)
  local copies, waits for them, and re-layouts  60.4 us (5%)
  matrix products  34.5 us (3%)
  between operations  14.5 us (1%)
    reduce_scatter x1, waiting for transfers between devices, on_device(): lax.psum_scatter(ordered, ('gx', 'gy'), scatter_dimension=0, tiled=True)  703 us
    psum x1, waiting for transfers between devices, on_device(): lax.psum(jnp.dot(owned.T, owned, precision=lax.Precision.HIGHEST, preferr...  169 us
    all_gather x1, waiting for transfers between devices, on_device(): terms = lax.all_gather(local_gram, ('gx', 'gy'), axis=0, tiled=False)  140 us
  transfers between devices with their start and end apart: 3, of which 3 were waited for; matrix products, arithmetic and copies ran while one was open for 0% of the time, Pallas kernels for 0%

profile of v1, /device:TPU:1, one launch (start us, length us, event | category | flops | bytes accessed | tf_op | source)
XLA Modules:
  0.0 1213.1 jit_solution(5570681264958211143)
XLA Ops:
  7.9 2.5 broadcast_in_dim.44
  10.4 47.0 %while.20 = (s32[]{:T(128)}, f32[64,128,128]{2,1,0:T(8,128)}, s32[]{:T(128)}, s32[192]{0:T(256)S(1)}, s32[]{:T(128)}, /*index=5*/bf16[192,128,128]{2,1,0:T(8,128...) while((s32[]{:T(128)}, f32[64,128,128]{2,1,0:T(8,128)}, ...), condition=%wide.region_2.3_spmd, body=%wide.region_0.2_spmd.sunk | while | flops 67634312 | bytes 6296211 | solution.py:35
  10.5 4.0 gather_fusion
  15.2 1.3 convolution_select_fusion.4
  16.5 3.3 scatter_fusion
  19.9 4.0 gather_fusion
  24.6 1.3 convolution_select_fusion.4
  25.9 3.2 scatter_fusion
  29.3 4.0 gather_fusion
  34.0 1.3 convolution_select_fusion.4
  35.3 3.2 scatter_fusion
  38.6 4.0 gather_fusion
  43.3 1.3 convolution_select_fusion.4
  44.7 3.3 scatter_fusion
  48.1 4.0 gather_fusion
  52.8 1.3 convolution_select_fusion.4
  54.1 3.3 scatter_fusion
  57.4 10.8 convolution_bitcast_fusion
  68.5 139.9 %all-gather.3.cloned.1.call-done = f32[16384,128]{1,0:T(8,128)} async-done(((f32[128,128]{1,0:T(8,128)}), f32[16384,128]{1,0:T(8,128)}) %all-gather.3.cloned.1.call-update) | async-done | bytes 8388624 | tf_op jit(solution)/shard_map/all_gather | solution.py:40
  208.5 3.8 reduce_sum.9
  212.4 11.7 cholesky.44
  225.4 9.8 custom-call.8
  235.3 6.2 fusion.4
  241.4 7.8 broadcast_in_dim.45
  249.3 39.0 %while.21 = (s32[]{:T(128)}, f32[256,128,128]{2,1,0:T(8,128)}, s32[]{:T(128)}, s32[192]{0:T(256)S(1)}, s32[]{:T(128)}, /*index=5*/bf16[192,128,128]{2,1,0:T(8,12...) while((s32[]{:T(128)}, f32[256,128,128]{2,1,0:T(8,128)}, ...), condition=%wide.region_8.10_spmd, body=%wide.region_6.9_spmd.sunk | while | flops 67634312 | bytes 6296211 | solution.py:60
  249.3 2.2 gather_fusion.1
  252.2 1.4 convolution_select_fusion.5
  253.7 3.4 scatter_fusion.1
  257.2 2.2 gather_fusion.1
  260.1 1.4 convolution_select_fusion.5
  261.5 3.4 scatter_fusion.1
  264.9 2.2 gather_fusion.1
  267.8 1.4 convolution_select_fusion.5
  269.3 3.4 scatter_fusion.1
  272.7 2.2 gather_fusion.1
  275.6 1.4 convolution_select_fusion.5
  277.0 3.4 scatter_fusion.1
  280.5 2.2 gather_fusion.1
  283.4 1.4 convolution_select_fusion.5
  284.8 3.4 scatter_fusion.1
  288.2 17.7 %gather_fusion.2 = f32[256,128,128]{2,1,0:T(8,128)} fusion(f32[256,128,128]{2,1,0:T(8,128)} %get-tuple-element.90, s32[1024]{0:T(1024)S(1)} %pad_clamp_fusion.2), kind=kCustom, calls=%fused_computation.2 | custom fusion | bytes 33555456 | tf_op jit(solution)/shard_map/gather | solution.py:63
  306.0 703.1 %reduce-scatter.2.cloned.1.call-done = f32[256,128]{1,0:T(8,128)} async-done(((f32[32768,128]{1,0:T(8,128)}), f32[256,128]{1,0:T(8,128)}) %reduce-scatter.2.cloned.1.call-update) | async-done | bytes 131088 | tf_op jit(solution)/shard_map/reduce_scatter | solution.py:64
  1009.1 2.0 fusion.11
  1011.1 169.0 %all-reduce.2.cloned.1.call-done = f32[128,128]{0,1:T(8,128)} async-done(((f32[128,128]{0,1:T(8,128)}), f32[128,128]{0,1:T(8,128)}) %all-reduce.2.cloned.1.call-update) | async-done | bytes 65552 | tf_op jit(solution)/shard_map/psum | solution.py:65
  1180.1 0.9 copy.17
  1181.9 11.7 cholesky.55
  1195.0 9.8 custom-call.9
  1204.8 1.8 convolution_multiply_fusion.1
  (53 shorter events, 11.4 us)
Async XLA Ops:
  7.2 3.2 copy-start
  7.2 3.2 copy-start.1
  7.2 201.3 %all-gather.3.cloned.1.call-start = ((), (), s32[]{:S(2)}) async-start(), calls=%async_computation.3 | async-start | bytes 8454144 | tf_op jit(solution)/shard_map/all_gather | solution.py:40
  57.4 11.1 copy-start.2
  68.3 940.8 %reduce-scatter.2.cloned.1.call-start = ((), (), s32[]{:S(2)}) async-start(), calls=%async_computation.1 | async-start | bytes 16908288 | tf_op jit(solution)/shard_map/reduce_scatter | solution.py:64
  305.9 874.2 %all-reduce.2.cloned.1.call-start = ((), (), s32[]{:S(2)}) async-start(), calls=%async_computation.2 | async-start | bytes 131072 | tf_op jit(solution)/shard_map/psum | solution.py:65
Sparse Core Ops, SparseCore 0:
  68.4 140.0 all-gather.2
  306.0 703.0 reduce-scatter.1
  1014.4 165.6 all-reduce.1
